TPU v7x, 32 devices: a whole 2x2x4 slice. The times are simulated.
32 devices in a mesh: group: 2 (over y), seq: 4 (over z), head: 4 (over x, core).
Axes of the slice: x: 2, y: 2, z: 4, core: 2. Of those that a mesh axis runs over, the one named last changes fastest.
Arguments:
- tokens: bfloat16 [4096, 768], P(('group', 'seq')), parts along dimension 0, may hold values from -40 to 40
- w_qkv: bfloat16 [3, 768, 768], P(None, None, 'head'), may hold values from -1 to 1
- w_out: bfloat16 [768, 768], P('head'), may hold values from -0.75 to 0.75
- gain: float32 [768], P('head'), may hold values from 0.5 to 1.5
- bias: float32 [768], P('head'), may hold values from -3 to 3
- mid_offset: int32 [12], P('head'), may hold values from 0 to 7
- far_offset: int32 [12], P('head'), may hold values from 0 to 31
Outputs:
- encoded: bfloat16 [4096, 768], P(('group', 'seq'), 'head'), parts along dimension 0
There are 2 independent parts, one for each index of `group`. A program takes and returns all parts, laid end to end along the dimension named above; an argument that names none is the same for every part. Nothing has to cross between parts.
All inputs are finite; a program needn't handle non-finite values.
Results may differ from a plain program's by a relative error of at most 0.0085.
Values may be sent and summed in bfloat16 or wider, within the bound.
No kernel may reach another device: no remote copies, remote signals or barrier semaphores. Data moves between devices by JAX's collectives and lax.ppermute only.
A program may use at most 64 MiB of HBM per device.

v0:
```python
from functools import partial
import math
import jax
import jax.numpy as jnp
from jax import lax
from jax.sharding import PartitionSpec as P

HEADS = 12
SEG0 = 128
R1 = 8
R2 = 32
epsilon = 1e-05


def attend(queries, keys_in, values_in, scale):
    scores = (
        jnp.einsum("qhd,khd->hqk", queries, keys_in, preferred_element_type=jnp.float32) * scale
    )
    peaks = jnp.max(scores, axis=-1)
    shifted = jnp.exp(scores - peaks[..., None])
    masses = jnp.sum(shifted, axis=-1)
    weights = shifted.astype(jnp.bfloat16)
    summed = jnp.einsum("hqk,khd->qhd", weights, values_in, preferred_element_type=jnp.float32)
    result = summed / jnp.transpose(masses)[:, :, None]
    log_mass = jnp.transpose(peaks + jnp.log(masses))
    return (result, log_mass)


def pick(source, offset, rate):
    folded = source.reshape(source.shape[0] // rate, rate, source.shape[1], source.shape[2])
    chosen = lax.broadcasted_iota(jnp.int32, (rate, source.shape[1]), 0) == offset[None, :]
    kept = jnp.where(chosen[None, :, :, None], folded, jnp.zeros((), source.dtype))
    return jnp.sum(kept, axis=1)


def spread(result, log_mass, offset, rate):
    count = result.shape[0]
    chosen = lax.broadcasted_iota(jnp.int32, (rate, result.shape[1]), 0) == offset[None, :]
    full = jnp.where(chosen[None, :, :, None], result[:, None], 0.0)
    full = full.reshape(count * rate, result.shape[1], result.shape[2])
    mass_full = jnp.where(chosen[None], log_mass[:, None, :], -1e30).reshape(
        count * rate, result.shape[1]
    )
    return (full, mass_full)


def local(tokens, w_qkv, w_out, gain, bias, mid_offset, far_offset):
    rows_here = tokens.shape[0]
    width = tokens.shape[1]
    heads_here = mid_offset.shape[0]
    head_size = width // HEADS
    cols_here = heads_here * head_size
    scale = 1.0 / math.sqrt(head_size)
    projected = jnp.einsum("td,sde->ste", tokens, w_qkv, preferred_element_type=jnp.float32).astype(
        jnp.bfloat16
    )
    query = projected[0].reshape(rows_here, heads_here, head_size)
    keyed = projected[1].reshape(rows_here, heads_here, head_size)
    value = projected[2].reshape(rows_here, heads_here, head_size)
    blocks = rows_here // SEG0
    near_out, near_mass = jax.vmap(partial(attend, scale=scale))(
        query.reshape(blocks, SEG0, heads_here, head_size),
        keyed.reshape(blocks, SEG0, heads_here, head_size),
        value.reshape(blocks, SEG0, heads_here, head_size),
    )
    near_out = near_out.reshape(rows_here, heads_here, head_size)
    near_mass = near_mass.reshape(rows_here, heads_here)
    mid_count = rows_here // R1
    far_count = rows_here // R2
    mid_query = pick(query, mid_offset, R1)
    mid_stack = jnp.stack(
        [
            pick(keyed, mid_offset, R1).reshape(mid_count, cols_here),
            pick(value, mid_offset, R1).reshape(mid_count, cols_here),
        ]
    )
    far_query = pick(query, far_offset, R2)
    far_stack = jnp.stack(
        [
            pick(keyed, far_offset, R2).reshape(far_count, cols_here),
            pick(value, far_offset, R2).reshape(far_count, cols_here),
        ]
    )
    mid_devs = min(8, lax.axis_size("seq"))
    place = lax.axis_index("seq")
    gathered_mid, far_all = (
        lax.all_gather(mid_stack, "seq", axis=1, tiled=True),
        lax.all_gather(far_stack, "seq", axis=1, tiled=True),
    )
    first_row = place // mid_devs * (mid_devs * mid_count)
    mid_all = lax.dynamic_slice_in_dim(gathered_mid, first_row, mid_devs * mid_count, 1)
    mid_out, mid_mass = attend(
        mid_query,
        mid_all[0].reshape(-1, heads_here, head_size),
        mid_all[1].reshape(-1, heads_here, head_size),
        scale,
    )
    far_out, far_mass = attend(
        far_query,
        far_all[0].reshape(-1, heads_here, head_size),
        far_all[1].reshape(-1, heads_here, head_size),
        scale,
    )
    mid_full, mid_mfull = spread(mid_out, mid_mass, mid_offset, R1)
    far_full, far_mfull = spread(far_out, far_mass, far_offset, R2)
    top = jnp.maximum(jnp.maximum(near_mass, mid_mfull), far_mfull)
    near_weight = jnp.exp(near_mass - top)
    mid_weight = jnp.exp(mid_mfull - top)
    far_weight = jnp.exp(far_mfull - top)
    mixed = (
        near_weight[..., None] * near_out
        + mid_weight[..., None] * mid_full
        + far_weight[..., None] * far_full
    )
    mixed = mixed / (near_weight + mid_weight + far_weight)[..., None]
    attn = mixed.reshape(rows_here, cols_here).astype(jnp.bfloat16)
    head_count = lax.axis_size("head")
    head_place = lax.axis_index("head")
    piece_cols = width // head_count
    weight_cols = lax.all_to_all(w_out, "head", split_axis=1, concat_axis=0, tiled=True)
    summed = jnp.dot(
        lax.all_gather(attn, "head", axis=1, tiled=True),
        weight_cols,
        preferred_element_type=jnp.float32,
    )
    resid = (
        lax.dynamic_slice_in_dim(tokens, head_place * piece_cols, piece_cols, 1).astype(jnp.float32)
        + summed
    )
    totals, squares = lax.psum((jnp.sum(resid, axis=1), jnp.sum(resid * resid, axis=1)), "head")
    mean = totals / width
    var = squares / width - mean * mean
    normed_cols = (resid - mean[:, None]) * lax.rsqrt(var + epsilon)[:, None]
    return (normed_cols * gain + bias).astype(jnp.bfloat16)


def solution(mesh):
    in_specs = (
        P(("group", "seq"), None),
        P(None, None, "head"),
        P("head", None),
        P("head"),
        P("head"),
        P("head"),
        P("head"),
    )
    out_specs = P(("group", "seq"), "head")
    return jax.shard_map(local, mesh=mesh, in_specs=in_specs, out_specs=out_specs, check_vma=False)
```

profile of v0, /device:TPU:0, one launch (start us, length us, event | category | flops | bytes accessed | tf_op | source)
XLA Modules:
  0.0 76.6 jit_solution(17679054772339913622)
XLA Ops:
  0.0 2.0 %copy.128 = bf16[192,768]{0,1:T(8,128)(2,1)} copy(bf16[192,768]{1,0:T(8,128)(2,1)} %param.9) | data formatting | bytes 589824 | tf_op args[2]
  2.0 4.2 %all-to-all-start = ((bf16[192,4,192]{0,2,1:T(8,128)(2,1)}), bf16[192,4,192]{0,2,1:T(8,128)(2,1)}, u32[]{:S(2)}, u32[]{:S(2)}) async-start(bf16[192,4,192]{0,2,1:T(8,128)(2,1)} %bitcast.24), calls=%async_computation | async-start | bytes 786432 | tf_op jit(solution)/shard_map/all_to_all | solution.py:120
  6.2 0.7 fusion
  7.0 0.1 copy.103
  7.1 0.1 reshape_reshape_squeeze.29
  7.3 0.1 reshape_reshape_squeeze.32
  7.4 0.1 copy.104
  7.7 1.0 %reshape_reshape_squeeze.30 = bf16[64,8,3,64]{3,2,1,0:T(4,128)(2,1)} reshape(bf16[1,512,192]{2,1,0:T(8,128)(2,1)S(1)} %copy.104) | data formatting | bytes 393216 | tf_op jit(solution)/shard_map/reshape;reshape;squeeze | solution.py:30
  8.7 0.1 reshape_reshape_squeeze.33
  8.8 0.1 copy.106
  9.0 0.9 %reshape_reshape_squeeze.31 = bf16[64,8,3,64]{3,2,1,0:T(4,128)(2,1)} reshape(bf16[1,512,192]{2,1,0:T(8,128)(2,1)S(1)} %copy.106) | data formatting | bytes 393216 | tf_op jit(solution)/shard_map/reshape;reshape;squeeze | solution.py:30
  9.9 0.1 reshape_reshape_squeeze.34
  10.1 1.7 %reshape_reshape_squeeze.27 = bf16[4,128,3,64]{1,0,3,2:T(4,128)(2,1)} reshape(bf16[1,512,192]{1,2,0:T(8,128)(2,1)} %copy-done.4) | data formatting | bytes 393216 | tf_op jit(solution)/shard_map/reshape;reshape;squeeze | solution.py:62
  11.8 1.7 %reshape_reshape_squeeze.28 = bf16[4,128,3,64]{1,0,3,2:T(4,128)(2,1)} reshape(bf16[1,512,192]{1,2,0:T(8,128)(2,1)} %copy-done.3) | data formatting | bytes 393216 | tf_op jit(solution)/shard_map/reshape;reshape;squeeze | solution.py:63
  13.4 1.7 %reshape_reshape_squeeze.35 = bf16[4,128,3,64]{1,0,3,2:T(4,128)(2,1)} reshape(bf16[1,512,192]{1,2,0:T(8,128)(2,1)} %copy-done.2) | data formatting | bytes 393216 | tf_op jit(solution)/shard_map/reshape;reshape;squeeze | solution.py:64
  15.1 0.1 copy.102
  15.2 3.4 %select_reduce_fusion.5 = (bf16[64,3,64]{2,1,0:T(4,128)(2,1)}, bf16[64,3,64]{2,1,0:T(4,128)(2,1)}, bf16[64,3,64]{2,1,0:T(4,128)(2,1)}) fusion(bf16[64,8,3,64]{3,2,1,0:T(4,128)(2,1)S(1)} %reshape_reshape_squeeze.29, pred[8,3]{1,0:T(8,128)(4,1)S(1)} %iota_compare_fusion.1, bf16[64,8,3,64]{3,2,1,0:T(4,128)(2,1)S(1)} %copy-done.1, ...), kind=kLoop, calls=%fused_computation.21 | loop fusion | flops 552960 | bytes 663576 | tf_op jit(solution)/shard_map/reduce_sum | solution.py:33
  18.6 0.9 %copy.105 = bf16[64,3,64]{0,2,1:T(8,128)(2,1)S(1)} copy(bf16[64,3,64]{2,1,0:T(4,128)(2,1)} %get-tuple-element.11) | data formatting | bytes 49152 | tf_op jit(solution)/shard_map/reduce_sum | solution.py:33
  19.5 0.9 %copy.107 = bf16[64,3,64]{0,2,1:T(8,128)(2,1)S(1)} copy(bf16[64,3,64]{2,1,0:T(4,128)(2,1)} %get-tuple-element.12) | data formatting | bytes 49152 | tf_op jit(solution)/shard_map/reduce_sum | solution.py:33
  20.5 0.1 copy.108
  20.6 15.6 %all_gather.9 = bf16[2,256,192]{2,0,1:T(2,128)(2,1)S(1)} all-gather(bf16[2,64,192]{2,0,1:T(2,128)(2,1)S(1)} %copy.108), channel_id=1, replica_groups=mesh['group'=2,'seq'=4,'head'=4] {'seq'}, dimensions={1}, use_global_device_ids=true | all-gather | bytes 245760 | tf_op jit(solution)/shard_map/all_gather | solution.py:87
  36.2 0.4 fusion.31
  36.6 0.1 copy.109
  36.8 0.2 fusion.34
  37.0 0.2 fusion.17
  37.3 0.1 broadcast_in_dim.173
  37.4 0.1 copy.111
  37.5 1.1 %select_reduce_fusion.2 = (bf16[16,3,64]{2,1,0:T(4,128)(2,1)S(1)}, bf16[16,3,64]{2,1,0:T(4,128)(2,1)S(1)}, bf16[16,3,64]{2,1,0:T(4,128)(2,1)S(1)}) fusion(bf16[16,32,3,64]{3,2,1,0:T(4,128)(2,1)S(1)} %reshape_reshape_squeeze.32, pred[32,3]{1,0:T(8,128)(4,1)S(1)} %iota_compare_fusion, bf16[16,32,3,64]{3,2,1,0:T(4,128)(2,1)S(1)} %reshape_reshape_squeeze.33, ...), kind=kLoop, calls=%fused_computation.18 | loop fusion | flops 580608 | bytes 608352 | tf_op jit(solution)/shard_map/reduce_sum | solution.py:33
  38.7 0.1 stack_reshape.14
  38.8 0.1 stack_reshape.15
  38.9 13.3 %all_gather.10 = bf16[2,64,192]{2,1,0:T(8,128)(2,1)S(1)} all-gather(bf16[2,16,192]{2,1,0:T(8,128)(2,1)S(1)} %pad_maximum_fusion.1), channel_id=1, replica_groups=mesh['group'=2,'seq'=4,'head'=4] {'seq'}, dimensions={1}, use_global_device_ids=true | all-gather | bytes 61440 | tf_op jit(solution)/shard_map/all_gather | solution.py:88
  52.2 0.1 copy.115
  52.3 0.2 fusion.33
  52.5 0.2 fusion.22
  52.8 0.1 broadcast_in_dim.180
  52.9 0.1 broadcast_in_dim.169
  53.0 0.1 broadcast_in_dim.176
  53.1 0.1 copy.121
  53.3 0.2 fusion.2
  53.5 0.1 copy.122
  53.6 0.1 broadcast_in_dim.183
  53.8 0.6 broadcast_in_dim.184
  54.3 0.2 copy.123
  54.5 0.1 copy.124
  54.6 0.2 fusion.3
  54.9 0.1 broadcast_in_dim.188
  55.0 0.6 broadcast_in_dim.189
  55.6 0.2 copy.127
  55.8 0.2 copy-done.5
  56.0 0.1 copy-done.6
  56.1 0.3 fusion.35
  56.4 0.1 fusion.6
  56.5 0.5 copy-done.8
  57.0 0.3 fusion.1
  57.2 0.3 copy.120
  57.5 1.1 %constant_dynamic-slice_fusion = bf16[512,192]{1,0:T(8,128)(2,1)S(1)} fusion(bf16[512,768]{1,0:T(8,128)(2,1)} %param.7, s32[]{:T(128)S(6)} %select_n.99), kind=kLoop, calls=%fused_computation.61 | loop fusion | bytes 393220 | tf_op jit(solution)/shard_map/dynamic_slice | solution.py:127
  58.6 0.1 copy.133
  58.8 0.2 fusion.12
  59.0 8.8 %all_gather.11 = bf16[512,768]{0,1:T(8,128)(2,1)S(1)} all-gather(bf16[512,192]{0,1:T(8,128)(2,1)S(1)} %fusion.12), channel_id=1, replica_groups=mesh['group'=2,'seq'=4,'head'=4] {'head'}, dimensions={1}, use_global_device_ids=true | all-gather | bytes 983040 | tf_op jit(solution)/shard_map/all_gather | solution.py:122
  67.8 1.3 %copy.129 = bf16[4,192,192]{1,0,2:T(4,128)(2,1)S(1)} copy(bf16[4,192,192]{1,2,0:T(8,128)(2,1)} %bitcast.25) | data formatting | bytes 589824 | tf_op jit(solution)/shard_map/all_to_all | solution.py:120
  69.1 0.3 all_to_all.17
  69.4 0.3 fusion.28
  69.8 6.0 %all-reduce = (f32[512]{0:T(512)S(1)}, f32[512]{0:T(512)S(1)}) all-reduce(f32[512]{0:T(512)S(1)} %get-tuple-element.6, f32[512]{0:T(512)S(1)} %get-tuple-element.5), channel_id=1, replica_groups=mesh['group'=2,'seq'=4,'head'=4] {'head'}, use_global_device_ids=true, to_apply=%region_15.16 | all-reduce | flops 1024 | bytes 8192 | tf_op jit(solution)/shard_map/psum | solution.py:130
  75.8 0.8 %add_convert_fusion = bf16[512,192]{0,1:T(8,128)(2,1)} fusion(f32[512,192]{0,1:T(8,128)S(1)} %get-tuple-element.34, f32[192]{0:T(256)S(1)} %copy-done.10, f32[192]{0:T(256)S(1)} %copy-done.11, f32[512]{0:T(512)S(1)} %get-tuple-element.27, f32[512]{0:T(512)S(1)} %get-tuple-element.26), kind=kLoop, calls=%fused_computation.28 | loop fusion | flops 491520 | bytes 595456 | tf_op jit(solution)/shard_map/convert_element_type | solution.py:134
  (41 shorter events, 0.5 us)
Async XLA Ops:
  0.0 6.2 %copy-start = (bf16[3,768,192]{1,2,0:T(8,128)(2,1)S(1)}, bf16[3,768,192]{1,2,0:T(8,128)(2,1)}, u32[]{:S(2)}) copy-start(bf16[3,768,192]{1,2,0:T(8,128)(2,1)} %param.8) | copy-start | bytes 2654212
  0.0 6.2 %copy-start.9 = (bf16[512,768]{1,0:T(8,128)(2,1)S(1)}, bf16[512,768]{1,0:T(8,128)(2,1)}, u32[]{:S(2)}) copy-start(bf16[512,768]{1,0:T(8,128)(2,1)} %param.7) | copy-start | bytes 2359300
  2.0 65.7 %all-to-all-start = ((bf16[192,4,192]{0,2,1:T(8,128)(2,1)}), bf16[192,4,192]{0,2,1:T(8,128)(2,1)}, u32[]{:S(2)}, u32[]{:S(2)}) async-start(bf16[192,4,192]{0,2,1:T(8,128)(2,1)} %bitcast.24), calls=%async_computation | async-start | bytes 786432 | tf_op jit(solution)/shard_map/all_to_all | solution.py:120
  6.9 0.7 copy-start.3
  7.0 0.7 copy-start.4
  7.0 1.8 %copy-start.2 = (bf16[1,512,192]{1,2,0:T(8,128)(2,1)}, bf16[1,512,192]{1,2,0:T(8,128)(2,1)S(1)}, u32[]{:S(2)}) copy-start(bf16[1,512,192]{1,2,0:T(8,128)(2,1)S(1)} %get-tuple-element.19) | copy-start | bytes 589828
  9.9 5.2 %copy-start.13 = (s32[3]{0:T(128)S(1)}, s32[3]{0:T(128)}, u32[]{:S(2)}) copy-start(s32[3]{0:T(128)} %param.12) | copy-start | bytes 40
  10.0 5.1 %copy-start.1 = (bf16[64,8,3,64]{3,2,1,0:T(4,128)(2,1)S(1)}, bf16[64,8,3,64]{3,2,1,0:T(4,128)(2,1)}, u32[]{:S(2)}) copy-start(bf16[64,8,3,64]{3,2,1,0:T(4,128)(2,1)} %reshape_reshape_squeeze.30) | copy-start | bytes 589828
  20.5 16.3 %copy-start.7 = (bf16[64,3,64]{2,1,0:T(4,128)(2,1)S(1)}, bf16[64,3,64]{2,1,0:T(4,128)(2,1)}, u32[]{:S(2)}) copy-start(bf16[64,3,64]{2,1,0:T(4,128)(2,1)} %get-tuple-element.10) | copy-start | bytes 73732
  36.2 1.2 %copy-start.12 = (s32[3]{0:T(128)S(1)}, s32[3]{0:T(128)}, u32[]{:S(2)}) copy-start(s32[3]{0:T(128)} %param.13) | copy-start | bytes 40
  55.0 0.9 %copy-start.5 = (bf16[4,128,3,64]{1,0,3,2:T(4,128)(2,1)S(1)}, bf16[4,128,3,64]{1,0,3,2:T(4,128)(2,1)}, u32[]{:S(2)}) copy-start(bf16[4,128,3,64]{1,0,3,2:T(4,128)(2,1)} %reshape_reshape_squeeze.27) | copy-start | bytes 589828
  55.0 1.0 %copy-start.6 = (bf16[4,128,3,64]{1,0,3,2:T(4,128)(2,1)S(1)}, bf16[4,128,3,64]{1,0,3,2:T(4,128)(2,1)}, u32[]{:S(2)}) copy-start(bf16[4,128,3,64]{1,0,3,2:T(4,128)(2,1)} %reshape_reshape_squeeze.28) | copy-start | bytes 589828
  56.0 0.9 %copy-start.8 = (bf16[4,128,3,64]{1,0,3,2:T(4,128)(2,1)S(1)}, bf16[4,128,3,64]{1,0,3,2:T(4,128)(2,1)}, u32[]{:S(2)}) copy-start(bf16[4,128,3,64]{1,0,3,2:T(4,128)(2,1)} %reshape_reshape_squeeze.35) | copy-start | bytes 589828
  69.1 6.7 %copy-start.10 = (f32[192]{0:T(256)S(1)}, f32[192]{0:T(256)}, u32[]{:S(2)}) copy-start(f32[192]{0:T(256)} %param.11) | copy-start | bytes 2308
  69.1 6.7 %copy-start.11 = (f32[192]{0:T(256)S(1)}, f32[192]{0:T(256)}, u32[]{:S(2)}) copy-start(f32[192]{0:T(256)} %param.10) | copy-start | bytes 2308
where the time goes:
time: 77.2 us; the launch traced here: 76.6 us
  blocking collectives  43.7 us (57%)
  local copies, waits for them, and re-layouts  19.7 us (26%)
  other arithmetic  6.08 us (8%)
  starting transfers between devices  4.21 us (5%)
  matrix products  2.49 us (3%)
    all_gather x1, blocking collectives, local(): lax.all_gather(mid_stack, 'seq', axis=1, tiled=True)  15.6 us
    all_gather x1, blocking collectives, local(): lax.all_gather(far_stack, 'seq', axis=1, tiled=True)  13.3 us
    all_gather x1, blocking collectives, local(): lax.all_gather(attn, 'head', axis=1, tiled=True)  8.79 us
    psum x1, blocking collectives, local(): lax.psum((jnp.sum(resid, axis=1), jnp.sum(resid * resid, axis=1)), 'head')  6.01 us
    reduce_sum x2, other arithmetic, pick(): return jnp.sum(kept, axis=1)  4.51 us
    all_to_all x1, starting transfers between devices, local(): lax.all_to_all(w_out, 'head', split_axis=1, concat_axis=0, tiled=True)  4.21 us
    unnamed x30, local copies, waits for them, and re-layouts  3.03 us
    another operation x6, local copies, waits for them, and re-layouts, pick(): source.reshape(source.shape[0] // rate, rate, source.shape[1], source.sha...  2.48 us
  transfers between devices with their start and end apart: 1, of which 0 were waited for; matrix products, arithmetic and copies ran while one was open for 29% of the time, Pallas kernels for 0%

commit v1 on v0

--- a/solution.py
+++ b/solution.py
@@ -10,6 +10,27 @@
 R1 = 8
 R2 = 32
 epsilon = 1e-05
+
+
+def laid_out(blocks, dim):
+    blocks = jnp.moveaxis(blocks, 0, dim)
+    shape = blocks.shape
+    return blocks.reshape(*shape[:dim], shape[dim] * shape[dim + 1], *shape[dim + 2 :])
+
+
+def grow_blocks(shard, axis):
+    peers, position = (lax.axis_size(axis), lax.axis_index(axis))
+    blocks, stride = (shard[None], 1)
+    while stride < peers:
+        theirs = lax.ppermute(blocks, axis, [(i, i ^ stride) for i in range(peers)])
+        low = position & stride == 0
+        blocks = jnp.concatenate([jnp.where(low, blocks, theirs), jnp.where(low, theirs, blocks)])
+        stride *= 2
+    return blocks
+
+
+def doubled_up(x, axis, dim):
+    return laid_out(grow_blocks(x, axis), dim)
 
 
 def attend(queries, keys_in, values_in, scale):
@@ -84,7 +105,7 @@
     mid_devs = min(8, lax.axis_size("seq"))
     place = lax.axis_index("seq")
     gathered_mid, far_all = (
-        lax.all_gather(mid_stack, "seq", axis=1, tiled=True),
+        doubled_up(mid_stack, "seq", 1),
         lax.all_gather(far_stack, "seq", axis=1, tiled=True),
     )
     first_row = place // mid_devs * (mid_devs * mid_count)

time: 77.2 us -> 67.5 us (0.87)
  blocking collectives: 43.7 us -> 28.4 us
  waiting for transfers between devices: 0.01 us -> 5.3 us
  local copies, waits for them, and re-layouts: 19.7 us -> 14.6 us
  starting transfers between devices: 4.21 us -> 7.84 us
  matrix products: 2.49 us -> 4.38 us
    all_gather x1 -> x0, blocking collectives: 15.6 us -> none  [local(): lax.all_gather(mid_stack, 'seq', axis=1, tiled=True)]
    ppermute x0 -> x2, waiting for transfers between devices: none -> 5.3 us  [grow_blocks(): theirs = lax.ppermute(blocks, axis, [(i, i ^ stride) for i in range(peers)])]
    ppermute x0 -> x2, starting transfers between devices: none -> 3.74 us  [grow_blocks(): theirs = lax.ppermute(blocks, axis, [(i, i ^ stride) for i in range(peers)])]
    unnamed x30 -> x24, local copies, waits for them, and re-layouts: 3.03 us -> 5.14 us
    another operation x1, local copies, waits for them, and re-layouts: 1.71 us -> 0.05 us  [local(): query.reshape(blocks, SEG0, heads_here, head_size)]
    another operation x1, local copies, waits for them, and re-layouts: 1.66 us -> 0.05 us  [local(): keyed.reshape(blocks, SEG0, heads_here, head_size)]
    another operation x6, local copies, waits for them, and re-layouts: 2.48 us -> 0.87 us  [pick(): source.reshape(source.shape[0] // rate, rate, source.shape[1], source.sha...]
    another operation x1, local copies, waits for them, and re-layouts: 1.65 us -> 0.05 us  [local(): value.reshape(blocks, SEG0, heads_here, head_size)]
  transfers between devices with their start and end apart: 1 -> 3, of which waited for: 0 -> 1; matrix products, arithmetic and copies ran while one was open for 29% -> 19% of each run, Pallas kernels for 0% -> 0%
where the time goes in v1:
time: 67.5 us; the launch traced here: 66.9 us
  blocking collectives  28.4 us (42%)
  local copies, waits for them, and re-layouts  14.6 us (22%)
  starting transfers between devices  7.84 us (12%)
  other arithmetic  5.91 us (9%)
  waiting for transfers between devices  5.3 us (8%)
  matrix products  4.38 us (6%)
    all_gather x1, blocking collectives, local(): lax.all_gather(far_stack, 'seq', axis=1, tiled=True)  13.3 us
    all_gather x1, blocking collectives, local(): lax.all_gather(attn, 'head', axis=1, tiled=True)  9.07 us
    psum x1, blocking collectives, local(): lax.psum((jnp.sum(resid, axis=1), jnp.sum(resid * resid, axis=1)), 'head')  6.01 us
    ppermute x2, waiting for transfers between devices, grow_blocks(): theirs = lax.ppermute(blocks, axis, [(i, i ^ stride) for i in range(peers)])  5.3 us
    unnamed x24, local copies, waits for them, and re-layouts  5.14 us
    all_to_all x1, starting transfers between devices, local(): lax.all_to_all(w_out, 'head', split_axis=1, concat_axis=0, tiled=True)  4.1 us
    ppermute x2, starting transfers between devices, grow_blocks(): theirs = lax.ppermute(blocks, axis, [(i, i ^ stride) for i in range(peers)])  3.74 us
    reduce_sum x2, other arithmetic, pick(): return jnp.sum(kept, axis=1)  3.37 us
  transfers between devices with their start and end apart: 3, of which 1 were waited for; matrix products, arithmetic and copies ran while one was open for 19% of the time, Pallas kernels for 0%

profile of v1, /device:TPU:0, one launch (start us, length us, event | category | flops | bytes accessed | tf_op | source)
XLA Modules:
  0.0 66.9 jit_solution(11906557180900426708)
XLA Ops:
  0.0 1.2 %copy-done = bf16[3,768,192]{1,2,0:T(8,128)(2,1)S(1)} copy-done((bf16[3,768,192]{1,2,0:T(8,128)(2,1)S(1)}, bf16[3,768,192]{1,2,0:T(8,128)(2,1)}, u32[]{:S(2)}) %copy-start) | copy-done | bytes 884760
  1.2 1.8 %fusion = bf16[3,512,192]{1,2,0:T(8,128)(2,1)S(1)} fusion(bf16[3,768,192]{1,2,0:T(8,128)(2,1)S(1)} %copy-done, bf16[512,768]{1,0:T(8,128)(2,1)} %param.7), kind=kOutput, calls=%fused_computation.2 | convolution fusion | flops 453279744 | bytes 2260992 | tf_op jit(solution)/shard_map/td,sde->ste/dot_general | solution.py:75
  3.0 0.1 copy.78
  3.2 0.1 reshape_reshape_squeeze.29
  3.3 0.4 copy-done.3
  3.7 0.1 copy.79
  3.8 0.1 reshape_reshape_squeeze.30
  4.0 0.1 copy.81
  4.1 0.1 reshape_reshape_squeeze.31
  4.3 0.2 copy-done.10
  4.5 2.3 %select_reduce_fusion.5 = (bf16[64,3,64]{2,1,0:T(4,128)(2,1)}, bf16[64,3,64]{2,1,0:T(4,128)(2,1)}, bf16[64,3,64]{2,1,0:T(4,128)(2,1)S(1)}) fusion(bf16[64,8,3,64]{3,2,1,0:T(4,128)(2,1)S(1)} %reshape_reshape_squeeze.29, pred[8,3]{1,0:T(8,128)(4,1)S(1)} %iota_compare_fusion.1, bf16[64,8,3,64]{3,2,1,0:T(4,128)(2,1)S(1)} %reshape_reshape_squeeze.30, ...), kind=kLoop, calls=%fused_computation.21 | loop fusion | flops 552960 | bytes 663576 | tf_op jit(solution)/shard_map/reduce_sum | solution.py:54
  6.7 0.9 %copy.80 = bf16[64,3,64]{0,2,1:T(8,128)(2,1)S(1)} copy(bf16[64,3,64]{2,1,0:T(4,128)(2,1)} %get-tuple-element.11) | data formatting | bytes 49152 | tf_op jit(solution)/shard_map/reduce_sum | solution.py:54
  7.7 0.1 copy.82
  7.8 0.1 copy.83
  7.9 3.1 %collective-permute-start = (bf16[1,2,64,192]{3,2,1,0:T(8,128)(2,1)S(1)}, bf16[1,2,64,192]{3,2,1,0:T(8,128)(2,1)}, u32[]{:S(2)}, u32[]{:S(2)}) collective-permute-start(bf16[1,2,64,192]{3,2,1,0:T(8,128)(2,1)S(1)} %bitcast.121), channel_id=1, source_target_pairs={{0,4},{4,0},{8,12},{12,8},{1,5},{5,1},{9,13},{13,9},{2,6},{6,2},{1... | collective-permute-start | bytes 147464 | tf_op jit(solution)/shard_map/ppermute | solution.py:25
  11.0 1.9 %copy.103 = bf16[192,768]{0,1:T(8,128)(2,1)} copy(bf16[192,768]{1,0:T(8,128)(2,1)} %param.9) | data formatting | bytes 589824 | tf_op args[2]
  12.9 4.1 %all-to-all-start = ((bf16[192,4,192]{0,2,1:T(8,128)(2,1)}), bf16[192,4,192]{0,2,1:T(8,128)(2,1)}, u32[]{:S(2)}, u32[]{:S(2)}) async-start(bf16[192,4,192]{0,2,1:T(8,128)(2,1)} %bitcast.24), calls=%async_computation | async-start | bytes 786432 | tf_op jit(solution)/shard_map/all_to_all | solution.py:141
  17.0 0.1 reshape_reshape_squeeze.32
  17.2 0.1 reshape_reshape_squeeze.33
  17.3 0.1 reshape_reshape_squeeze.34
  17.5 0.4 copy-done.4
  18.0 0.1 copy-done.2
  18.3 1.1 %select_reduce_fusion.2 = (bf16[16,3,64]{2,1,0:T(4,128)(2,1)S(1)}, bf16[16,3,64]{2,1,0:T(4,128)(2,1)S(1)}, bf16[16,3,64]{2,1,0:T(4,128)(2,1)S(1)}) fusion(bf16[16,32,3,64]{3,2,1,0:T(4,128)(2,1)S(1)} %reshape_reshape_squeeze.32, pred[32,3]{1,0:T(8,128)(4,1)S(1)} %iota_compare_fusion, bf16[16,32,3,64]{3,2,1,0:T(4,128)(2,1)S(1)} %reshape_reshape_squeeze.33, ...), kind=kLoop, calls=%fused_computation.18 | loop fusion | flops 580608 | bytes 608352 | tf_op jit(solution)/shard_map/reduce_sum | solution.py:54
  19.6 13.3 %all_gather.6 = bf16[2,64,192]{2,1,0:T(8,128)(2,1)S(1)} all-gather(bf16[2,16,192]{2,1,0:T(8,128)(2,1)S(1)} %pad_maximum_fusion.2), channel_id=1, replica_groups=mesh['group'=2,'seq'=4,'head'=4] {'seq'}, dimensions={1}, use_global_device_ids=true | all-gather | bytes 61440 | tf_op jit(solution)/shard_map/all_gather | solution.py:109
  32.9 0.1 copy.90
  33.0 0.1 copy.99
  33.2 0.2 fusion.33
  33.4 0.2 fusion.22
  33.5 0.3 fusion.35
  33.9 0.1 fusion.6
  34.0 0.2 fusion.3
  34.2 1.0 %fusion.1 = f32[4,128,3,64]{1,3,2,0:T(8,128)} fusion(f32[4,3,128,128]{2,3,1,0:T(8,128)S(1)} %get-tuple-element.37, f32[4,3,128]{2,1,0:T(4,128)S(1)} %get-tuple-element.36, bf16[4,128,3,64]{1,0,3,2:T(4,128)(2,1)S(1)} %reshape_reshape_squeeze.35, f32[4,128,3]{1,2,0:T(4,128)S(1)} %bitcast.126), kind=kOutput, calls=%fused_computation.4 | convolution fusion | flops 25657344 | bytes 1388544 | tf_op jit(solution)/shard_map/vmap(hqk,khd->qhd)/dot_general | solution.py:44
  35.2 0.1 copy.77
  35.3 0.1 copy.86
  35.6 0.1 broadcast_in_dim.172
  35.9 0.1 broadcast_in_dim.192
  36.0 0.6 broadcast_in_dim.193
  36.6 0.2 copy.102
  36.8 0.8 %copy-done.5 = f32[4,128,3,64]{1,3,2,0:T(8,128)S(1)} copy-done((f32[4,128,3,64]{1,3,2,0:T(8,128)S(1)}, f32[4,128,3,64]{1,3,2,0:T(8,128)}, u32[]{:S(2)}) %copy-start.5) | copy-done | bytes 393240
  37.6 0.3 copy.95
  37.8 0.9 %broadcast_select_fusion.3 = (bf16[1,2,64,192]{3,2,1,0:T(8,128)(2,1)S(1)}, bf16[1,2,64,192]{3,2,1,0:T(8,128)(2,1)S(1)}) fusion(bf16[1,2,64,192]{3,2,1,0:T(8,128)(2,1)} %collective-permute-done, pred[]{:T(512)S(6)} %eq.31, bf16[2,64,192]{2,1,0:T(8,128)(2,1)S(1)} %copy.83), kind=kLoop, calls=%fused_computation.45 | loop fusion | flops 49152 | bytes 196609 | tf_op jit(solution)/shard_map/jit(_where)/select_n | solution.py:27
  38.7 0.7 collective-permute-start.1
  39.4 1.1 %constant_dynamic-slice_fusion = bf16[512,192]{1,0:T(8,128)(2,1)S(1)} fusion(bf16[512,768]{1,0:T(8,128)(2,1)} %param.7, s32[]{:T(128)S(6)} %select_n.123), kind=kLoop, calls=%fused_computation.67 | loop fusion | bytes 393220 | tf_op jit(solution)/shard_map/dynamic_slice | solution.py:148
  40.5 0.1 copy.108
  40.7 5.3 %collective-permute-done.1 = bf16[2,2,64,192]{3,2,1,0:T(8,128)(2,1)S(1)} collective-permute-done((bf16[2,2,64,192]{3,2,1,0:T(8,128)(2,1)S(1)}, bf16[2,2,64,192]{3,2,1,0:T(8,128)(2,1)S(1)}, u32[]{:S(2)}, u32[]{:S(2)}) %collective-permute-start.1) | collective-permute-done | bytes 98336 | tf_op jit(solution)/shard_map/ppermute | solution.py:25
  46.1 0.2 copy.84
  46.3 0.2 reshape_squeeze.12
  46.5 0.2 fusion.34
  46.7 0.2 fusion.17
  47.0 0.1 broadcast_in_dim.177
  47.1 0.2 copy.96
  47.3 0.2 reshape_squeeze.14
  47.5 0.2 fusion.2
  47.7 0.1 copy.97
  47.8 0.1 broadcast_in_dim.187
  48.0 0.6 broadcast_in_dim.188
  48.5 0.2 copy.98
  48.8 0.2 fusion.12
  48.9 9.1 %all_gather.7 = bf16[512,768]{0,1:T(8,128)(2,1)S(1)} all-gather(bf16[512,192]{0,1:T(8,128)(2,1)S(1)} %fusion.12), channel_id=1, replica_groups=mesh['group'=2,'seq'=4,'head'=4] {'head'}, dimensions={1}, use_global_device_ids=true | all-gather | bytes 983040 | tf_op jit(solution)/shard_map/all_gather | solution.py:143
  58.0 1.3 %copy.104 = bf16[4,192,192]{1,0,2:T(4,128)(2,1)S(1)} copy(bf16[4,192,192]{1,2,0:T(8,128)(2,1)} %bitcast.25) | data formatting | bytes 589824 | tf_op jit(solution)/shard_map/all_to_all | solution.py:141
  59.3 0.3 all_to_all.17
  59.7 0.4 fusion.28
  60.0 6.0 %all-reduce = (f32[512]{0:T(512)S(1)}, f32[512]{0:T(512)S(1)}) all-reduce(f32[512]{0:T(512)S(1)} %get-tuple-element.6, f32[512]{0:T(512)S(1)} %get-tuple-element.5), channel_id=1, replica_groups=mesh['group'=2,'seq'=4,'head'=4] {'head'}, use_global_device_ids=true, to_apply=%region_15.16 | all-reduce | flops 1024 | bytes 8192 | tf_op jit(solution)/shard_map/psum | solution.py:151
  66.1 0.8 %add_convert_fusion = bf16[512,192]{0,1:T(8,128)(2,1)} fusion(f32[512,192]{0,1:T(8,128)S(1)} %get-tuple-element.38, f32[192]{0:T(256)S(1)} %copy-done.7, f32[192]{0:T(256)S(1)} %copy-done.8, f32[512]{0:T(512)S(1)} %get-tuple-element.31, f32[512]{0:T(512)S(1)} %get-tuple-element.30), kind=kLoop, calls=%fused_computation.28 | loop fusion | flops 491520 | bytes 595456 | tf_op jit(solution)/shard_map/convert_element_type | solution.py:155
  (44 shorter events, 1.0 us)
Async XLA Ops:
  0.0 1.2 %copy-start = (bf16[3,768,192]{1,2,0:T(8,128)(2,1)S(1)}, bf16[3,768,192]{1,2,0:T(8,128)(2,1)}, u32[]{:S(2)}) copy-start(bf16[3,768,192]{1,2,0:T(8,128)(2,1)} %param.8) | copy-start | bytes 2654212
  3.0 0.7 %copy-start.3 = (bf16[1,512,192]{1,2,0:T(8,128)(2,1)}, bf16[1,512,192]{1,2,0:T(8,128)(2,1)S(1)}, u32[]{:S(2)}) copy-start(bf16[1,512,192]{1,2,0:T(8,128)(2,1)S(1)} %get-tuple-element.21) | copy-start | bytes 589828
  3.0 1.0 %copy-start.1 = (bf16[1,512,192]{1,2,0:T(8,128)(2,1)}, bf16[1,512,192]{1,2,0:T(8,128)(2,1)S(1)}, u32[]{:S(2)}) copy-start(bf16[1,512,192]{1,2,0:T(8,128)(2,1)S(1)} %get-tuple-element.20) | copy-start | bytes 589828
  3.8 0.7 copy-start.10
  7.9 29.9 %collective-permute-start = (bf16[1,2,64,192]{3,2,1,0:T(8,128)(2,1)S(1)}, bf16[1,2,64,192]{3,2,1,0:T(8,128)(2,1)}, u32[]{:S(2)}, u32[]{:S(2)}) collective-permute-start(bf16[1,2,64,192]{3,2,1,0:T(8,128)(2,1)S(1)} %bitcast.121), channel_id=1, source_target_pairs={{0,4},{4,0},{8,12},{12,8},{1,5},{5,1},{9,13},{13,9},{2,6},{6,2},{1... | collective-permute-start | bytes 147464 | tf_op jit(solution)/shard_map/ppermute | solution.py:25
  12.9 45.1 %all-to-all-start = ((bf16[192,4,192]{0,2,1:T(8,128)(2,1)}), bf16[192,4,192]{0,2,1:T(8,128)(2,1)}, u32[]{:S(2)}, u32[]{:S(2)}) async-start(bf16[192,4,192]{0,2,1:T(8,128)(2,1)} %bitcast.24), calls=%async_computation | async-start | bytes 786432 | tf_op jit(solution)/shard_map/all_to_all | solution.py:141
  17.0 0.9 %copy-start.4 = (bf16[1,512,192]{1,2,0:T(8,128)(2,1)S(1)}, bf16[1,512,192]{1,2,0:T(8,128)(2,1)}, u32[]{:S(2)}) copy-start(bf16[1,512,192]{1,2,0:T(8,128)(2,1)} %copy-done.3) | copy-start | bytes 589828
  17.2 1.0 %copy-start.2 = (bf16[1,512,192]{1,2,0:T(8,128)(2,1)S(1)}, bf16[1,512,192]{1,2,0:T(8,128)(2,1)}, u32[]{:S(2)}) copy-start(bf16[1,512,192]{1,2,0:T(8,128)(2,1)} %copy-done.1) | copy-start | bytes 589828
  17.3 0.9 %copy-start.9 = (s32[3]{0:T(128)S(1)}, s32[3]{0:T(128)}, u32[]{:S(2)}) copy-start(s32[3]{0:T(128)} %param.13) | copy-start | bytes 40
  36.6 1.0 %copy-start.5 = (f32[4,128,3,64]{1,3,2,0:T(8,128)S(1)}, f32[4,128,3,64]{1,3,2,0:T(8,128)}, u32[]{:S(2)}) copy-start(f32[4,128,3,64]{1,3,2,0:T(8,128)} %fusion.1) | copy-start | bytes 1179652
  38.7 7.2 %collective-permute-start.1 = (bf16[2,2,64,192]{3,2,1,0:T(8,128)(2,1)S(1)}, bf16[2,2,64,192]{3,2,1,0:T(8,128)(2,1)S(1)}, u32[]{:S(2)}, u32[]{:S(2)}) collective-permute-start(bf16[2,2,64,192]{3,2,1,0:T(8,128)(2,1)S(1)} %pad_maximum_fusion), channel_id=1, source_target_pairs={{0,8},{4,12},{8,0},{12,4},{1,9},{5,13},{9,1},{13,5},{2,10},{6,14},... | collective-permute-start | bytes 294920 | tf_op jit(solution)/shard_map/ppermute | solution.py:25
  40.7 5.8 %copy-start.6 = (bf16[64,3,64]{2,1,0:T(4,128)(2,1)S(1)}, bf16[64,3,64]{2,1,0:T(4,128)(2,1)}, u32[]{:S(2)}) copy-start(bf16[64,3,64]{2,1,0:T(4,128)(2,1)} %get-tuple-element.10) | copy-start | bytes 73732
  59.3 6.8 %copy-start.7 = (f32[192]{0:T(256)S(1)}, f32[192]{0:T(256)}, u32[]{:S(2)}) copy-start(f32[192]{0:T(256)} %param.11) | copy-start | bytes 2308
  59.3 6.7 %copy-start.8 = (f32[192]{0:T(256)S(1)}, f32[192]{0:T(256)}, u32[]{:S(2)}) copy-start(f32[192]{0:T(256)} %param.10) | copy-start | bytes 2308
